TPU v7x, 512 devices: a whole 4x8x8 slice. The times are simulated.
512 devices in a mesh: rows: 64 (over x, y, core), cols: 8 (over z).
Axes of the slice: x: 4, y: 8, z: 8, core: 2. Of those that a mesh axis runs over, the one named last changes fastest.
Arguments:
- eigvecs: float32 [65536, 2048], P(('rows', 'cols')), may hold values from -6 to 6
- panels: float32 [8, 65536, 256], P('cols', 'rows'), may hold values from -0.375 to 0.375
- tfactors: float32 [2, 256, 256], replicated, may hold values from -0.03125 to 0.03125
- owners: int32 [2], replicated, may hold values from 0 to 7, as said below
Outputs:
- backvecs: float32 [65536, 2048], P('rows', 'cols')
Inputs may be any that keep to these rules, and one draw needn't show every extreme that they name: `owners`: the entries are distinct slots, among them 0 and 7.
All inputs are finite; a program needn't handle non-finite values.
Results may differ from a plain program's by a relative error of at most 0.00011.
Values sent between devices are 32-bit elements; how exact they have to be, the bound alone decides.
No kernel may reach another device: no remote copies, remote signals or barrier semaphores. Data moves between devices by JAX's collectives and lax.ppermute only.
A program may use at most 64 MiB of HBM per device.

v0:
```python
import jax
import jax.numpy as jnp
from jax import lax
from jax.sharding import Mesh, PartitionSpec as P

PLANE = ("x", "y")


def dot(left, right, dims):
    return lax.dot_general(
        left,
        right,
        (dims, ((), ())),
        precision=lax.Precision.HIGH,
        preferred_element_type=jnp.float32,
    )


def tn(left, right):
    return dot(left, right, ((0,), (0,)))


def nn(left, right):
    return dot(left, right, ((1,), (0,)))


def shift(value, by):
    count = lax.axis_size("z")
    return lax.ppermute(value, "z", [(slot, (slot + by) % count) for slot in range(count)])


def owner_quarters(local):
    quarter = local.shape[0] // 4
    last = lax.axis_index("z") == lax.axis_size("z") - 1
    starts = [jnp.where(last, (3 - step) * quarter, step * quarter) for step in range(4)]
    return [lax.dynamic_slice_in_dim(local, start, quarter) for start in starts]


def scatter_quarters(pieces):
    slot = lax.axis_index("z")
    last = lax.axis_size("z") - 1
    chunk = pieces[0]
    for step in range(1, 4):
        piece = lax.ppermute(pieces[step], "z", [(0, step), (last, last - step)])
        chunk = jnp.where((slot == step) | (slot == last - step), piece, chunk)
    return chunk


def gather_panels(chunk):
    rows, width = chunk.shape
    before2, after2 = (shift(chunk, 2), shift(chunk, -2))
    before1, after1 = (shift(chunk, 1), shift(chunk, -1))
    after3, before3 = (shift(after2, -1), shift(before2, 1))
    across = jnp.concatenate([shift(after2[: rows // 2], -2), shift(before2[rows // 2 :], 2)])
    before, after = ([chunk, before1, before2, before3], [chunk, after1, after2, after3])
    slot = lax.axis_index("z")
    both = jnp.zeros((8, rows, width), chunk.dtype)
    for by, piece in enumerate(before):
        both = lax.dynamic_update_index_in_dim(both, piece, (slot - by) % 8, 0)
    for by, piece in enumerate(after[1:]):
        both = lax.dynamic_update_index_in_dim(both, piece, (slot + by + 1) % 8, 0)
    both = lax.dynamic_update_index_in_dim(both, across, (slot + 4) % 8, 0)
    return both.reshape(2, 4 * rows, width)


def products(first, second, tiles, half):
    width = tiles.shape[1] // 2
    tiles, other = (
        lax.dynamic_slice_in_dim(value, half * width, width, 1) for value in (tiles, first)
    )
    return jnp.concatenate([tn(first, tiles), tn(second, tiles), tn(second, other)])


def reduce_rows(first, second, tiles):
    core = lax.axis_index("c")
    other = products(first, second, tiles, 1 - core)
    other = lax.ppermute(other, "c", [(0, 1), (1, 0)])
    part = products(first, second, tiles, core) + other
    rows, columns = part.shape
    planes = lax.axis_size("x") * lax.axis_size("y")
    pieces = part.reshape(planes, rows // planes, columns)
    pieces = lax.all_to_all(pieces, PLANE, split_axis=0, concat_axis=0, tiled=True)
    pieces = jnp.broadcast_to(pieces.sum(0)[None], pieces.shape)
    pieces = lax.all_to_all(pieces, PLANE, split_axis=0, concat_axis=0, tiled=True)
    return lax.all_gather(pieces.reshape(rows, columns), "c", axis=1, tiled=True)


def per_device(eigvecs, panels, tfactors, owners):
    pieces = owner_quarters(panels[0])
    pieces, eigvecs = lax.optimization_barrier((pieces, eigvecs))
    chunk = scatter_quarters(pieces)
    factors = jnp.triu(tfactors)
    count = lax.axis_size("z")
    tiles = eigvecs.reshape(eigvecs.shape[0], count, -1).swapaxes(0, 1)
    chunk, tiles, factors = lax.optimization_barrier((chunk, tiles, factors))
    tiles = lax.all_to_all(tiles, "z", split_axis=0, concat_axis=0, tiled=True)
    tiles = tiles.reshape(-1, tiles.shape[2])
    both = gather_panels(chunk)
    lead = jnp.where(owners[0] == 0, 0, 1)
    first = lax.dynamic_index_in_dim(both, lead, 0, False)
    second = lax.dynamic_index_in_dim(both, 1 - lead, 0, False)
    width = first.shape[1]
    total = reduce_rows(first, second, tiles)
    proj_first, proj_second, cross = (total[:width], total[width : 2 * width], total[2 * width :])
    coeff_first = nn(factors[0], proj_first)
    coeff_second = nn(factors[1], proj_second - nn(cross, coeff_first))
    return tiles - nn(first, coeff_first) - nn(second, coeff_second)


def solution(mesh):
    split = Mesh(mesh.devices.reshape(4, 8, 2, 8), ("x", "y", "c", "z"))
    rows = ("x", "y", "c")
    placed = (P(rows + ("z",), None), P("z", rows, None), P(), P())
    return jax.shard_map(
        per_device, mesh=split, in_specs=placed, out_specs=P(rows, "z"), check_vma=False
    )
```

profile of v0, /device:TPU:1, one launch (start us, length us, event | category | flops | bytes accessed | tf_op | source)
XLA Modules:
  0.0 146.7 jit_solution(18208789601227877676)
XLA Ops:
  0.0 1.4 dynamic-slice_bitcast_fusion
  1.4 8.5 %collective-permute-start = (f32[256,256]{1,0:T(8,128)S(1)}, f32[256,256]{1,0:T(8,128)S(1)}, u32[]{:S(2)}, u32[]{:S(2)}) collective-permute-start(f32[256,256]{1,0:T(8,128)S(1)} %get-tuple-element.13), channel_id=1, source_target_pairs={{0,3},{7,4},{8,11},{15,12},{16,19},{23,20},{24,27},{31,28},{32,35}... | collective-permute-start | bytes 786440 | tf_op jit(solution)/shard_map/ppermute | solution.py:44
  9.9 2.0 %collective-permute-start.1 = (f32[256,256]{1,0:T(8,128)S(1)}, f32[256,256]{1,0:T(8,128)}, u32[]{:S(2)}, u32[]{:S(2)}) collective-permute-start(f32[256,256]{1,0:T(8,128)S(1)} %get-tuple-element.14), channel_id=1, source_target_pairs={{0,2},{7,5},{8,10},{15,13},{16,18},{23,21},{24,26},{31,29},{32,34}... | collective-permute-start | bytes 786440 | tf_op jit(solution)/shard_map/ppermute | solution.py:44
  11.9 2.0 %collective-permute-start.2 = (f32[256,256]{1,0:T(8,128)S(1)}, f32[256,256]{1,0:T(8,128)}, u32[]{:S(2)}, u32[]{:S(2)}) collective-permute-start(f32[256,256]{1,0:T(8,128)S(1)} %get-tuple-element.15), channel_id=1, source_target_pairs={{0,1},{7,6},{8,9},{15,14},{16,17},{23,22},{24,25},{31,30},{32,33},... | collective-permute-start | bytes 786440 | tf_op jit(solution)/shard_map/ppermute | solution.py:44
  14.0 1.1 copy.8
  15.9 4.5 %collective-permute-done.1 = f32[256,256]{1,0:T(8,128)} collective-permute-done((f32[256,256]{1,0:T(8,128)S(1)}, f32[256,256]{1,0:T(8,128)}, u32[]{:S(2)}, u32[]{:S(2)}) %collective-permute-start.1) | collective-permute-done | bytes 262176 | tf_op jit(solution)/shard_map/ppermute | solution.py:44
  20.4 5.6 %collective-permute-done.2 = f32[256,256]{1,0:T(8,128)} collective-permute-done((f32[256,256]{1,0:T(8,128)S(1)}, f32[256,256]{1,0:T(8,128)}, u32[]{:S(2)}, u32[]{:S(2)}) %collective-permute-start.2) | collective-permute-done | bytes 262176 | tf_op jit(solution)/shard_map/ppermute | solution.py:44
  26.1 1.9 %collective-permute-start.4 = (f32[256,256]{1,0:T(8,128)S(1)}, f32[256,256]{1,0:T(8,128)}, u32[]{:S(2)}, u32[]{:S(2)}) collective-permute-start(f32[256,256]{1,0:T(8,128)S(1)} %select_select_fusion), channel_id=1, source_target_pairs={{0,2},{1,3},{2,4},{3,5},{4,6},{5,7},{6,0},{7,1},{8,10},{9,11},{10,... | collective-permute-start | bytes 786440 | tf_op jit(solution)/shard_map/ppermute | solution.py:29
  28.0 8.2 %collective-permute-start.7 = (f32[256,256]{1,0:T(8,128)S(1)}, f32[256,256]{1,0:T(8,128)}, u32[]{:S(2)}, u32[]{:S(2)}) collective-permute-start(f32[256,256]{1,0:T(8,128)S(1)} %select_select_fusion), channel_id=1, source_target_pairs={{0,6},{1,7},{2,0},{3,1},{4,2},{5,3},{6,4},{7,5},{8,14},{9,15},{10,... | collective-permute-start | bytes 786440 | tf_op jit(solution)/shard_map/ppermute | solution.py:29
  36.2 2.5 %collective-permute-start.3 = (f32[256,256]{1,0:T(8,128)S(1)}, f32[256,256]{1,0:T(8,128)}, u32[]{:S(2)}, u32[]{:S(2)}) collective-permute-start(f32[256,256]{1,0:T(8,128)S(1)} %select_select_fusion), channel_id=1, source_target_pairs={{0,1},{1,2},{2,3},{3,4},{4,5},{5,6},{6,7},{7,0},{8,9},{9,10},{10,1... | collective-permute-start | bytes 786440 | tf_op jit(solution)/shard_map/ppermute | solution.py:29
  38.9 4.0 %collective-permute-start.6 = (f32[256,256]{1,0:T(8,128)S(1)}, f32[256,256]{1,0:T(8,128)}, u32[]{:S(2)}, u32[]{:S(2)}) collective-permute-start(f32[256,256]{1,0:T(8,128)S(1)} %select_select_fusion), channel_id=1, source_target_pairs={{0,7},{1,0},{2,1},{3,2},{4,3},{5,4},{6,5},{7,6},{8,15},{9,8},{10,9... | collective-permute-start | bytes 786440 | tf_op jit(solution)/shard_map/ppermute | solution.py:29
  42.9 3.6 %all-to-all-start = ((f32[8,128,256]{2,1,0:T(8,128)}), f32[8,128,256]{2,1,0:T(8,128)S(1)}, u32[]{:S(2)}, u32[]{:S(2)}) async-start(f32[8,128,256]{2,1,0:T(8,128)} %bitcast.71), calls=%async_computation | async-start | bytes 2097152 | tf_op jit(solution)/shard_map/all_to_all | solution.py:96
  47.6 4.2 %collective-permute-start.10 = (f32[128,256]{1,0:T(8,128)S(1)}, f32[128,256]{1,0:T(8,128)S(1)}, u32[]{:S(2)}, u32[]{:S(2)}) collective-permute-start(f32[128,256]{1,0:T(8,128)S(1)} %slice.33), channel_id=1, source_target_pairs={{0,2},{1,3},{2,4},{3,5},{4,6},{5,7},{6,0},{7,1},{8,10},{9,11},{10,... | collective-permute-start | bytes 393224 | tf_op jit(solution)/shard_map/ppermute | solution.py:29
  52.8 3.2 %collective-permute-start.9 = (f32[128,256]{1,0:T(8,128)S(1)}, f32[128,256]{1,0:T(8,128)S(1)}, u32[]{:S(2)}, u32[]{:S(2)}) collective-permute-start(f32[128,256]{1,0:T(8,128)S(1)} %slice.32), channel_id=1, source_target_pairs={{0,6},{1,7},{2,0},{3,1},{4,2},{5,3},{6,4},{7,5},{8,14},{9,15},{10,... | collective-permute-start | bytes 393224 | tf_op jit(solution)/shard_map/ppermute | solution.py:29
  56.0 3.3 %collective-permute-start.5 = (f32[256,256]{1,0:T(8,128)}, f32[256,256]{1,0:T(8,128)S(1)}, u32[]{:S(2)}, u32[]{:S(2)}) collective-permute-start(f32[256,256]{1,0:T(8,128)} %collective-permute-done.4), channel_id=1, source_target_pairs={{0,1},{1,2},{2,3},{3,4},{4,5},{5,6},{6,7},{7,0},{8,9},{9,10},{10,1... | collective-permute-start | bytes 786440 | tf_op jit(solution)/shard_map/ppermute | solution.py:29
  59.3 3.2 %collective-permute-start.8 = (f32[256,256]{1,0:T(8,128)}, f32[256,256]{1,0:T(8,128)S(1)}, u32[]{:S(2)}, u32[]{:S(2)}) collective-permute-start(f32[256,256]{1,0:T(8,128)} %collective-permute-done.7), channel_id=1, source_target_pairs={{0,7},{1,0},{2,1},{3,2},{4,3},{5,4},{6,5},{7,6},{8,15},{9,8},{10,9... | collective-permute-start | bytes 786440 | tf_op jit(solution)/shard_map/ppermute | solution.py:29
  64.5 20.9 %collective-permute-done.5 = f32[256,256]{1,0:T(8,128)S(1)} collective-permute-done((f32[256,256]{1,0:T(8,128)}, f32[256,256]{1,0:T(8,128)S(1)}, u32[]{:S(2)}, u32[]{:S(2)}) %collective-permute-start.5) | collective-permute-done | bytes 262176 | tf_op jit(solution)/shard_map/ppermute | solution.py:29
  87.4 1.2 fusion.1
  91.4 2.4 %collective-permute-start.11 = (f32[768,128]{1,0:T(8,128)}, f32[768,128]{1,0:T(8,128)S(1)}, u32[]{:S(2)}, u32[]{:S(2)}) collective-permute-start(f32[768,128]{1,0:T(8,128)} %pad_maximum_fusion), channel_id=1, source_target_pairs={{0,8},{8,0},{1,9},{9,1},{2,10},{10,2},{3,11},{11,3},{4,12},{12,4},... | collective-permute-start | bytes 1179656 | tf_op jit(solution)/shard_map/ppermute | solution.py:77
  93.8 1.2 fusion.5
  97.1 21.7 %all_to_all.15 = f32[32,24,128]{2,1,0:T(8,128)S(1)} all-to-all(f32[32,24,128]{2,1,0:T(8,128)S(1)} %bitcast.86), channel_id=1, replica_groups=mesh['x'=4,'y'=8,'c'=2,'z'=8] {'x','y'}, dimensions={0} | all-to-all | bytes 786432 | tf_op jit(solution)/shard_map/all_to_all | solution.py:82
  118.9 18.6 %all_to_all.16 = f32[32,24,128]{2,1,0:T(8,128)S(1)} all-to-all(f32[32,24,128]{2,1,0:T(8,128)S(1)} %broadcast_in_dim.53), channel_id=1, replica_groups=mesh['x'=4,'y'=8,'c'=2,'z'=8] {'x','y'}, dimensions={0} | all-to-all | bytes 786432 | tf_op jit(solution)/shard_map/all_to_all | solution.py:84
  137.5 6.2 %all_gather.3 = f32[768,256]{1,0:T(8,128)S(1)} all-gather(f32[768,128]{1,0:T(8,128)S(1)} %bitcast.87), channel_id=1, replica_groups=mesh['x'=4,'y'=8,'c'=2,'z'=8] {'c'}, dimensions={1}, use_global_device_ids=true | all-gather | bytes 1179648 | tf_op jit(solution)/shard_map/all_gather | solution.py:85
  145.1 1.6 %convolution_subtract_fusion = f32[1024,256]{1,0:T(8,128)} fusion(f32[1024,256]{1,0:T(8,128)S(1)} %convolution_subtract_fusion.1, f32[256,256]{1,0:T(8,128)S(1)} %fusion.34, f32[2,1024,256]{2,1,0:T(8,128)S(1)} %bitcast.80, s32[]{:T(128)S(6)} %select_n.156), kind=kOutput, calls=%fused_computation | convolution fusion | flops 402915328 | bytes 3407876 | tf_op jit(solution)/shard_map/dot_general | solution.py:10
  (45 shorter events, 13.4 us)
Async XLA Ops:
  0.0 14.0 %copy-start.1 = (f32[128,2048]{1,0:T(8,128)S(1)}, f32[128,2048]{1,0:T(8,128)}, u32[]{:S(2)}) copy-start(f32[128,2048]{1,0:T(8,128)} %param.4) | copy-start | bytes 3145732
  0.0 15.1 %copy-start.2 = (f32[2,256,256]{2,1,0:T(8,128)S(1)}, f32[2,256,256]{2,1,0:T(8,128)}, u32[]{:S(2)}) copy-start(f32[2,256,256]{2,1,0:T(8,128)} %param.6) | copy-start | bytes 1572868
  1.4 14.5 %collective-permute-start = (f32[256,256]{1,0:T(8,128)S(1)}, f32[256,256]{1,0:T(8,128)S(1)}, u32[]{:S(2)}, u32[]{:S(2)}) collective-permute-start(f32[256,256]{1,0:T(8,128)S(1)} %get-tuple-element.13), channel_id=1, source_target_pairs={{0,3},{7,4},{8,11},{15,12},{16,19},{23,20},{24,27},{31,28},{32,35}... | collective-permute-start | bytes 786440 | tf_op jit(solution)/shard_map/ppermute | solution.py:44
  9.9 10.6 %collective-permute-start.1 = (f32[256,256]{1,0:T(8,128)S(1)}, f32[256,256]{1,0:T(8,128)}, u32[]{:S(2)}, u32[]{:S(2)}) collective-permute-start(f32[256,256]{1,0:T(8,128)S(1)} %get-tuple-element.14), channel_id=1, source_target_pairs={{0,2},{7,5},{8,10},{15,13},{16,18},{23,21},{24,26},{31,29},{32,34}... | collective-permute-start | bytes 786440 | tf_op jit(solution)/shard_map/ppermute | solution.py:44
  11.9 14.2 %collective-permute-start.2 = (f32[256,256]{1,0:T(8,128)S(1)}, f32[256,256]{1,0:T(8,128)}, u32[]{:S(2)}, u32[]{:S(2)}) collective-permute-start(f32[256,256]{1,0:T(8,128)S(1)} %get-tuple-element.15), channel_id=1, source_target_pairs={{0,1},{7,6},{8,9},{15,14},{16,17},{23,22},{24,25},{31,30},{32,33},... | collective-permute-start | bytes 786440 | tf_op jit(solution)/shard_map/ppermute | solution.py:44
  14.0 24.8 %copy-start.3 = (s32[2]{0:T(128)S(1)}, s32[2]{0:T(128)}, u32[]{:S(2)}) copy-start(s32[2]{0:T(128)} %param.7) | copy-start | bytes 28
  26.1 20.6 %collective-permute-start.4 = (f32[256,256]{1,0:T(8,128)S(1)}, f32[256,256]{1,0:T(8,128)}, u32[]{:S(2)}, u32[]{:S(2)}) collective-permute-start(f32[256,256]{1,0:T(8,128)S(1)} %select_select_fusion), channel_id=1, source_target_pairs={{0,2},{1,3},{2,4},{3,5},{4,6},{5,7},{6,0},{7,1},{8,10},{9,11},{10,... | collective-permute-start | bytes 786440 | tf_op jit(solution)/shard_map/ppermute | solution.py:29
  28.0 23.8 %collective-permute-start.7 = (f32[256,256]{1,0:T(8,128)S(1)}, f32[256,256]{1,0:T(8,128)}, u32[]{:S(2)}, u32[]{:S(2)}) collective-permute-start(f32[256,256]{1,0:T(8,128)S(1)} %select_select_fusion), channel_id=1, source_target_pairs={{0,6},{1,7},{2,0},{3,1},{4,2},{5,3},{6,4},{7,5},{8,14},{9,15},{10,... | collective-permute-start | bytes 786440 | tf_op jit(solution)/shard_map/ppermute | solution.py:29
  36.2 23.0 %collective-permute-start.3 = (f32[256,256]{1,0:T(8,128)S(1)}, f32[256,256]{1,0:T(8,128)}, u32[]{:S(2)}, u32[]{:S(2)}) collective-permute-start(f32[256,256]{1,0:T(8,128)S(1)} %select_select_fusion), channel_id=1, source_target_pairs={{0,1},{1,2},{2,3},{3,4},{4,5},{5,6},{6,7},{7,0},{8,9},{9,10},{10,1... | collective-permute-start | bytes 786440 | tf_op jit(solution)/shard_map/ppermute | solution.py:29
  38.9 46.5 %collective-permute-start.6 = (f32[256,256]{1,0:T(8,128)S(1)}, f32[256,256]{1,0:T(8,128)}, u32[]{:S(2)}, u32[]{:S(2)}) collective-permute-start(f32[256,256]{1,0:T(8,128)S(1)} %select_select_fusion), channel_id=1, source_target_pairs={{0,7},{1,0},{2,1},{3,2},{4,3},{5,4},{6,5},{7,6},{8,15},{9,8},{10,9... | collective-permute-start | bytes 786440 | tf_op jit(solution)/shard_map/ppermute | solution.py:29
  42.9 45.7 %all-to-all-start = ((f32[8,128,256]{2,1,0:T(8,128)}), f32[8,128,256]{2,1,0:T(8,128)S(1)}, u32[]{:S(2)}, u32[]{:S(2)}) async-start(f32[8,128,256]{2,1,0:T(8,128)} %bitcast.71), calls=%async_computation | async-start | bytes 2097152 | tf_op jit(solution)/shard_map/all_to_all | solution.py:96
  47.6 39.7 %collective-permute-start.10 = (f32[128,256]{1,0:T(8,128)S(1)}, f32[128,256]{1,0:T(8,128)S(1)}, u32[]{:S(2)}, u32[]{:S(2)}) collective-permute-start(f32[128,256]{1,0:T(8,128)S(1)} %slice.33), channel_id=1, source_target_pairs={{0,2},{1,3},{2,4},{3,5},{4,6},{5,7},{6,0},{7,1},{8,10},{9,11},{10,... | collective-permute-start | bytes 393224 | tf_op jit(solution)/shard_map/ppermute | solution.py:29
  52.8 34.6 %collective-permute-start.9 = (f32[128,256]{1,0:T(8,128)S(1)}, f32[128,256]{1,0:T(8,128)S(1)}, u32[]{:S(2)}, u32[]{:S(2)}) collective-permute-start(f32[128,256]{1,0:T(8,128)S(1)} %slice.32), channel_id=1, source_target_pairs={{0,6},{1,7},{2,0},{3,1},{4,2},{5,3},{6,4},{7,5},{8,14},{9,15},{10,... | collective-permute-start | bytes 393224 | tf_op jit(solution)/shard_map/ppermute | solution.py:29
  56.0 29.4 %collective-permute-start.5 = (f32[256,256]{1,0:T(8,128)}, f32[256,256]{1,0:T(8,128)S(1)}, u32[]{:S(2)}, u32[]{:S(2)}) collective-permute-start(f32[256,256]{1,0:T(8,128)} %collective-permute-done.4), channel_id=1, source_target_pairs={{0,1},{1,2},{2,3},{3,4},{4,5},{5,6},{6,7},{7,0},{8,9},{9,10},{10,1... | collective-permute-start | bytes 786440 | tf_op jit(solution)/shard_map/ppermute | solution.py:29
  59.3 28.1 %collective-permute-start.8 = (f32[256,256]{1,0:T(8,128)}, f32[256,256]{1,0:T(8,128)S(1)}, u32[]{:S(2)}, u32[]{:S(2)}) collective-permute-start(f32[256,256]{1,0:T(8,128)} %collective-permute-done.7), channel_id=1, source_target_pairs={{0,7},{1,0},{2,1},{3,2},{4,3},{5,4},{6,5},{7,6},{8,15},{9,8},{10,9... | collective-permute-start | bytes 786440 | tf_op jit(solution)/shard_map/ppermute | solution.py:29
  91.4 5.6 %collective-permute-start.11 = (f32[768,128]{1,0:T(8,128)}, f32[768,128]{1,0:T(8,128)S(1)}, u32[]{:S(2)}, u32[]{:S(2)}) collective-permute-start(f32[768,128]{1,0:T(8,128)} %pad_maximum_fusion), channel_id=1, source_target_pairs={{0,8},{8,0},{1,9},{9,1},{2,10},{10,2},{3,11},{11,3},{4,12},{12,4},... | collective-permute-start | bytes 1179656 | tf_op jit(solution)/shard_map/ppermute | solution.py:77
  118.8 24.9 %copy-start = (f32[2,256,256]{2,1,0:T(8,128)S(1)}, f32[2,256,256]{2,1,0:T(8,128)}, u32[]{:S(2)}) copy-start(f32[2,256,256]{2,1,0:T(8,128)} %broadcast_select_fusion) | copy-start | bytes 1572868
where the time goes:
time: 147 us
  starting transfers between devices  48.9 us (33%)
  blocking collectives  46.5 us (32%)
  waiting for transfers between devices  31 us (21%)
  matrix products  9.29 us (6%)
  local copies, waits for them, and re-layouts  8.46 us (6%)
  other arithmetic  1.9 us (1%)
    all_to_all x2, blocking collectives, reduce_rows(): lax.all_to_all(pieces, PLANE, split_axis=0, concat_axis=0, tiled=True)  40.3 us
    ppermute x8, starting transfers between devices, shift(): lax.ppermute(value, 'z', [(slot, (slot + by) % count) for slot in range(c...  30.5 us
    ppermute x8, waiting for transfers between devices, shift(): lax.ppermute(value, 'z', [(slot, (slot + by) % count) for slot in range(c...  20.9 us
    ppermute x3, starting transfers between devices, scatter_quarters(): piece = lax.ppermute(pieces[step], 'z', [(0, step), (last, last - step)])  12.5 us
    ppermute x3, waiting for transfers between devices, scatter_quarters(): piece = lax.ppermute(pieces[step], 'z', [(0, step), (last, last - step)])  10.1 us
    dot_general x11, matrix products, dot(): lax.dot_general(left, right, (dims, ((), ())), precision=lax.Precision.HI...  9.29 us
    all_gather x1, blocking collectives, reduce_rows(): lax.all_gather(pieces.reshape(rows, columns), 'c', axis=1, tiled=True)  6.22 us
    all_to_all x1, starting transfers between devices, per_device(): tiles = lax.all_to_all(tiles, 'z', split_axis=0, concat_axis=0, tiled=True)  3.57 us
  transfers between devices with their start and end apart: 13, of which 3 were waited for; matrix products, arithmetic and copies ran while one was open for 8% of the time, Pallas kernels for 0%

commit v1 on v0

--- a/solution.py
+++ b/solution.py
@@ -82,7 +82,10 @@
     pieces = lax.all_to_all(pieces, PLANE, split_axis=0, concat_axis=0, tiled=True)
     pieces = jnp.broadcast_to(pieces.sum(0)[None], pieces.shape)
     pieces = lax.all_to_all(pieces, PLANE, split_axis=0, concat_axis=0, tiled=True)
-    return lax.all_gather(pieces.reshape(rows, columns), "c", axis=1, tiled=True)
+    return jnp.concatenate(
+        lax.all_to_all(jnp.stack([pieces.reshape(rows, columns)] * lax.axis_size("c")), "c", 0, 0),
+        axis=1,
+    )
 
 
 def per_device(eigvecs, panels, tfactors, owners):

time: 147 us -> 156 us (1.061)
  local copies, waits for them, and re-layouts: 8.46 us -> 14.8 us
  blocking collectives: 46.5 us -> 48.4 us
    all_to_all x0 -> x1, blocking collectives: none -> 8.23 us  [reduce_rows(): lax.all_to_all(jnp.stack([pieces.reshape(rows, columns)] * lax.axis_size(...]
    all_gather x1 -> x0, blocking collectives: 6.22 us -> none  [reduce_rows(): lax.all_gather(pieces.reshape(rows, columns), 'c', axis=1, tiled=True)]
    slice x0 -> x5, local copies, waits for them, and re-layouts: none -> 5.66 us  [the longest x2 2.67 us: per_device(): total[2 * width:]]
where the time goes in v1:
time: 156 us
  blocking collectives  48.4 us (31%)
  starting transfers between devices  48.2 us (31%)
  waiting for transfers between devices  31 us (20%)
  local copies, waits for them, and re-layouts  14.8 us (9%)
  matrix products  10.5 us (7%)
  other arithmetic  1.95 us (1%)
    all_to_all x2, blocking collectives, reduce_rows(): lax.all_to_all(pieces, PLANE, split_axis=0, concat_axis=0, tiled=True)  40.2 us
    ppermute x8, starting transfers between devices, shift(): lax.ppermute(value, 'z', [(slot, (slot + by) % count) for slot in range(c...  30.5 us
    ppermute x8, waiting for transfers between devices, shift(): lax.ppermute(value, 'z', [(slot, (slot + by) % count) for slot in range(c...  20.9 us
    ppermute x3, starting transfers between devices, scatter_quarters(): piece = lax.ppermute(pieces[step], 'z', [(0, step), (last, last - step)])  11.8 us
    dot_general x11, matrix products, dot(): lax.dot_general(left, right, (dims, ((), ())), precision=lax.Precision.HI...  10.5 us
    ppermute x3, waiting for transfers between devices, scatter_quarters(): piece = lax.ppermute(pieces[step], 'z', [(0, step), (last, last - step)])  10.1 us
    all_to_all x1, blocking collectives, reduce_rows(): lax.all_to_all(jnp.stack([pieces.reshape(rows, columns)] * lax.axis_size(...  8.23 us
    all_to_all x1, starting transfers between devices, per_device(): tiles = lax.all_to_all(tiles, 'z', split_axis=0, concat_axis=0, tiled=True)  3.57 us
  transfers between devices with their start and end apart: 13, of which 3 were waited for; matrix products, arithmetic and copies ran while one was open for 8% of the time, Pallas kernels for 0%

profile of v1, /device:TPU:1, one launch (start us, length us, event | category | flops | bytes accessed | tf_op | source)
XLA Modules:
  0.0 155.5 jit_solution(17332426812511023034)
XLA Ops:
  0.0 1.4 dynamic-slice_bitcast_fusion
  1.4 8.5 %collective-permute-start = (f32[256,256]{1,0:T(8,128)S(1)}, f32[256,256]{1,0:T(8,128)S(1)}, u32[]{:S(2)}, u32[]{:S(2)}) collective-permute-start(f32[256,256]{1,0:T(8,128)S(1)} %get-tuple-element.13), channel_id=1, source_target_pairs={{0,3},{7,4},{8,11},{15,12},{16,19},{23,20},{24,27},{31,28},{32,35}... | collective-permute-start | bytes 786440 | tf_op jit(solution)/shard_map/ppermute | solution.py:44
  9.9 1.3 collective-permute-start.1
  11.2 2.0 %collective-permute-start.2 = (f32[256,256]{1,0:T(8,128)S(1)}, f32[256,256]{1,0:T(8,128)}, u32[]{:S(2)}, u32[]{:S(2)}) collective-permute-start(f32[256,256]{1,0:T(8,128)S(1)} %get-tuple-element.15), channel_id=1, source_target_pairs={{0,1},{7,6},{8,9},{15,14},{16,17},{23,22},{24,25},{31,30},{32,33},... | collective-permute-start | bytes 786440 | tf_op jit(solution)/shard_map/ppermute | solution.py:44
  15.2 5.2 %collective-permute-done.1 = f32[256,256]{1,0:T(8,128)S(1)} collective-permute-done((f32[256,256]{1,0:T(8,128)S(1)}, f32[256,256]{1,0:T(8,128)S(1)}, u32[]{:S(2)}, u32[]{:S(2)}) %collective-permute-start.1) | collective-permute-done | bytes 262176 | tf_op jit(solution)/shard_map/ppermute | solution.py:44
  21.1 4.9 %collective-permute-done.2 = f32[256,256]{1,0:T(8,128)} collective-permute-done((f32[256,256]{1,0:T(8,128)S(1)}, f32[256,256]{1,0:T(8,128)}, u32[]{:S(2)}, u32[]{:S(2)}) %collective-permute-start.2) | collective-permute-done | bytes 262176 | tf_op jit(solution)/shard_map/ppermute | solution.py:44
  26.1 1.9 %collective-permute-start.4 = (f32[256,256]{1,0:T(8,128)S(1)}, f32[256,256]{1,0:T(8,128)}, u32[]{:S(2)}, u32[]{:S(2)}) collective-permute-start(f32[256,256]{1,0:T(8,128)S(1)} %select_select_fusion), channel_id=1, source_target_pairs={{0,2},{1,3},{2,4},{3,5},{4,6},{5,7},{6,0},{7,1},{8,10},{9,11},{10,... | collective-permute-start | bytes 786440 | tf_op jit(solution)/shard_map/ppermute | solution.py:29
  28.0 8.2 %collective-permute-start.7 = (f32[256,256]{1,0:T(8,128)S(1)}, f32[256,256]{1,0:T(8,128)}, u32[]{:S(2)}, u32[]{:S(2)}) collective-permute-start(f32[256,256]{1,0:T(8,128)S(1)} %select_select_fusion), channel_id=1, source_target_pairs={{0,6},{1,7},{2,0},{3,1},{4,2},{5,3},{6,4},{7,5},{8,14},{9,15},{10,... | collective-permute-start | bytes 786440 | tf_op jit(solution)/shard_map/ppermute | solution.py:29
  36.2 2.5 %collective-permute-start.3 = (f32[256,256]{1,0:T(8,128)S(1)}, f32[256,256]{1,0:T(8,128)}, u32[]{:S(2)}, u32[]{:S(2)}) collective-permute-start(f32[256,256]{1,0:T(8,128)S(1)} %select_select_fusion), channel_id=1, source_target_pairs={{0,1},{1,2},{2,3},{3,4},{4,5},{5,6},{6,7},{7,0},{8,9},{9,10},{10,1... | collective-permute-start | bytes 786440 | tf_op jit(solution)/shard_map/ppermute | solution.py:29
  38.9 4.0 %collective-permute-start.6 = (f32[256,256]{1,0:T(8,128)S(1)}, f32[256,256]{1,0:T(8,128)}, u32[]{:S(2)}, u32[]{:S(2)}) collective-permute-start(f32[256,256]{1,0:T(8,128)S(1)} %select_select_fusion), channel_id=1, source_target_pairs={{0,7},{1,0},{2,1},{3,2},{4,3},{5,4},{6,5},{7,6},{8,15},{9,8},{10,9... | collective-permute-start | bytes 786440 | tf_op jit(solution)/shard_map/ppermute | solution.py:29
  42.9 3.6 %all-to-all-start = ((f32[8,128,256]{2,1,0:T(8,128)}), f32[8,128,256]{2,1,0:T(8,128)S(1)}, u32[]{:S(2)}, u32[]{:S(2)}) async-start(f32[8,128,256]{2,1,0:T(8,128)} %bitcast.77), calls=%async_computation | async-start | bytes 2097152 | tf_op jit(solution)/shard_map/all_to_all | solution.py:99
  47.6 4.2 %collective-permute-start.10 = (f32[128,256]{1,0:T(8,128)S(1)}, f32[128,256]{1,0:T(8,128)S(1)}, u32[]{:S(2)}, u32[]{:S(2)}) collective-permute-start(f32[128,256]{1,0:T(8,128)S(1)} %slice.45), channel_id=1, source_target_pairs={{0,2},{1,3},{2,4},{3,5},{4,6},{5,7},{6,0},{7,1},{8,10},{9,11},{10,... | collective-permute-start | bytes 393224 | tf_op jit(solution)/shard_map/ppermute | solution.py:29
  52.8 3.2 %collective-permute-start.9 = (f32[128,256]{1,0:T(8,128)S(1)}, f32[128,256]{1,0:T(8,128)S(1)}, u32[]{:S(2)}, u32[]{:S(2)}) collective-permute-start(f32[128,256]{1,0:T(8,128)S(1)} %slice.44), channel_id=1, source_target_pairs={{0,6},{1,7},{2,0},{3,1},{4,2},{5,3},{6,4},{7,5},{8,14},{9,15},{10,... | collective-permute-start | bytes 393224 | tf_op jit(solution)/shard_map/ppermute | solution.py:29
  56.0 3.3 %collective-permute-start.5 = (f32[256,256]{1,0:T(8,128)}, f32[256,256]{1,0:T(8,128)S(1)}, u32[]{:S(2)}, u32[]{:S(2)}) collective-permute-start(f32[256,256]{1,0:T(8,128)} %collective-permute-done.4), channel_id=1, source_target_pairs={{0,1},{1,2},{2,3},{3,4},{4,5},{5,6},{6,7},{7,0},{8,9},{9,10},{10,1... | collective-permute-start | bytes 786440 | tf_op jit(solution)/shard_map/ppermute | solution.py:29
  59.3 3.2 %collective-permute-start.8 = (f32[256,256]{1,0:T(8,128)}, f32[256,256]{1,0:T(8,128)S(1)}, u32[]{:S(2)}, u32[]{:S(2)}) collective-permute-start(f32[256,256]{1,0:T(8,128)} %collective-permute-done.7), channel_id=1, source_target_pairs={{0,7},{1,0},{2,1},{3,2},{4,3},{5,4},{6,5},{7,6},{8,15},{9,8},{10,9... | collective-permute-start | bytes 786440 | tf_op jit(solution)/shard_map/ppermute | solution.py:29
  64.5 20.9 %collective-permute-done.5 = f32[256,256]{1,0:T(8,128)S(1)} collective-permute-done((f32[256,256]{1,0:T(8,128)}, f32[256,256]{1,0:T(8,128)S(1)}, u32[]{:S(2)}, u32[]{:S(2)}) %collective-permute-start.5) | collective-permute-done | bytes 262176 | tf_op jit(solution)/shard_map/ppermute | solution.py:29
  87.4 1.2 fusion.1
  91.4 2.4 %collective-permute-start.11 = (f32[768,128]{1,0:T(8,128)}, f32[768,128]{1,0:T(8,128)S(1)}, u32[]{:S(2)}, u32[]{:S(2)}) collective-permute-start(f32[768,128]{1,0:T(8,128)} %pad_maximum_fusion.1), channel_id=1, source_target_pairs={{0,8},{8,0},{1,9},{9,1},{2,10},{10,2},{3,11},{11,3},{4,12},{12,4},... | collective-permute-start | bytes 1179656 | tf_op jit(solution)/shard_map/ppermute | solution.py:77
  97.1 21.7 %all_to_all.20 = f32[32,24,128]{2,1,0:T(8,128)S(1)} all-to-all(f32[32,24,128]{2,1,0:T(8,128)S(1)} %bitcast.93), channel_id=1, replica_groups=mesh['x'=4,'y'=8,'c'=2,'z'=8] {'x','y'}, dimensions={0} | all-to-all | bytes 786432 | tf_op jit(solution)/shard_map/all_to_all | solution.py:82
  118.9 18.5 %all_to_all.21 = f32[32,24,128]{2,1,0:T(8,128)S(1)} all-to-all(f32[32,24,128]{2,1,0:T(8,128)S(1)} %broadcast_in_dim.53), channel_id=1, replica_groups=mesh['x'=4,'y'=8,'c'=2,'z'=8] {'x','y'}, dimensions={0} | all-to-all | bytes 786432 | tf_op jit(solution)/shard_map/all_to_all | solution.py:84
  137.4 8.2 %all_to_all.22 = f32[2,768,128]{2,1,0:T(8,128)S(1)} all-to-all(f32[2,768,128]{2,1,0:T(8,128)S(1)} %pad_maximum_fusion), channel_id=1, replica_groups=mesh['x'=4,'y'=8,'c'=2,'z'=8] {'c'}, dimensions={0} | all-to-all | bytes 1572864 | tf_op jit(solution)/shard_map/all_to_all | solution.py:86
  149.5 1.8 %copy.10 = f32[256,2,128]{0,2,1:T(8,128)} copy(f32[256,2,128]{2,0,1:T(8,128)} %get-tuple-element.25) | data formatting | bytes 524288 | tf_op jit(solution)/shard_map/slice | solution.py:107
  151.3 1.3 fusion.33
  154.0 1.6 %convolution_subtract_fusion = f32[1024,256]{1,0:T(8,128)} fusion(f32[1024,256]{1,0:T(8,128)S(1)} %convolution_subtract_fusion.1, f32[256,256]{1,0:T(8,128)S(1)} %fusion.31, f32[2,1024,256]{2,1,0:T(8,128)S(1)} %bitcast.86, s32[]{:T(128)S(6)} %select_n.156), kind=kOutput, calls=%fused_computation | convolution fusion | flops 402915328 | bytes 3407876 | tf_op jit(solution)/shard_map/dot_general | solution.py:10
  (57 shorter events, 20.1 us)
Async XLA Ops:
  0.0 13.3 %copy-start.1 = (f32[128,2048]{1,0:T(8,128)S(1)}, f32[128,2048]{1,0:T(8,128)}, u32[]{:S(2)}) copy-start(f32[128,2048]{1,0:T(8,128)} %param.4) | copy-start | bytes 3145732
  0.0 14.4 %copy-start.4 = (f32[2,256,256]{2,1,0:T(8,128)S(1)}, f32[2,256,256]{2,1,0:T(8,128)}, u32[]{:S(2)}) copy-start(f32[2,256,256]{2,1,0:T(8,128)} %param.6) | copy-start | bytes 1572868
  1.4 13.9 %collective-permute-start = (f32[256,256]{1,0:T(8,128)S(1)}, f32[256,256]{1,0:T(8,128)S(1)}, u32[]{:S(2)}, u32[]{:S(2)}) collective-permute-start(f32[256,256]{1,0:T(8,128)S(1)} %get-tuple-element.13), channel_id=1, source_target_pairs={{0,3},{7,4},{8,11},{15,12},{16,19},{23,20},{24,27},{31,28},{32,35}... | collective-permute-start | bytes 786440 | tf_op jit(solution)/shard_map/ppermute | solution.py:44
  9.9 10.6 %collective-permute-start.1 = (f32[256,256]{1,0:T(8,128)S(1)}, f32[256,256]{1,0:T(8,128)S(1)}, u32[]{:S(2)}, u32[]{:S(2)}) collective-permute-start(f32[256,256]{1,0:T(8,128)S(1)} %get-tuple-element.14), channel_id=1, source_target_pairs={{0,2},{7,5},{8,10},{15,13},{16,18},{23,21},{24,26},{31,29},{32,34}... | collective-permute-start | bytes 786440 | tf_op jit(solution)/shard_map/ppermute | solution.py:44
  11.2 14.9 %collective-permute-start.2 = (f32[256,256]{1,0:T(8,128)S(1)}, f32[256,256]{1,0:T(8,128)}, u32[]{:S(2)}, u32[]{:S(2)}) collective-permute-start(f32[256,256]{1,0:T(8,128)S(1)} %get-tuple-element.15), channel_id=1, source_target_pairs={{0,1},{7,6},{8,9},{15,14},{16,17},{23,22},{24,25},{31,30},{32,33},... | collective-permute-start | bytes 786440 | tf_op jit(solution)/shard_map/ppermute | solution.py:44
  13.3 25.5 %copy-start.6 = (s32[2]{0:T(128)S(1)}, s32[2]{0:T(128)}, u32[]{:S(2)}) copy-start(s32[2]{0:T(128)} %param.7) | copy-start | bytes 28
  20.4 0.7 copy-start.5
  26.1 20.6 %collective-permute-start.4 = (f32[256,256]{1,0:T(8,128)S(1)}, f32[256,256]{1,0:T(8,128)}, u32[]{:S(2)}, u32[]{:S(2)}) collective-permute-start(f32[256,256]{1,0:T(8,128)S(1)} %select_select_fusion), channel_id=1, source_target_pairs={{0,2},{1,3},{2,4},{3,5},{4,6},{5,7},{6,0},{7,1},{8,10},{9,11},{10,... | collective-permute-start | bytes 786440 | tf_op jit(solution)/shard_map/ppermute | solution.py:29
  28.0 23.8 %collective-permute-start.7 = (f32[256,256]{1,0:T(8,128)S(1)}, f32[256,256]{1,0:T(8,128)}, u32[]{:S(2)}, u32[]{:S(2)}) collective-permute-start(f32[256,256]{1,0:T(8,128)S(1)} %select_select_fusion), channel_id=1, source_target_pairs={{0,6},{1,7},{2,0},{3,1},{4,2},{5,3},{6,4},{7,5},{8,14},{9,15},{10,... | collective-permute-start | bytes 786440 | tf_op jit(solution)/shard_map/ppermute | solution.py:29
  36.2 23.0 %collective-permute-start.3 = (f32[256,256]{1,0:T(8,128)S(1)}, f32[256,256]{1,0:T(8,128)}, u32[]{:S(2)}, u32[]{:S(2)}) collective-permute-start(f32[256,256]{1,0:T(8,128)S(1)} %select_select_fusion), channel_id=1, source_target_pairs={{0,1},{1,2},{2,3},{3,4},{4,5},{5,6},{6,7},{7,0},{8,9},{9,10},{10,1... | collective-permute-start | bytes 786440 | tf_op jit(solution)/shard_map/ppermute | solution.py:29
  38.9 46.5 %collective-permute-start.6 = (f32[256,256]{1,0:T(8,128)S(1)}, f32[256,256]{1,0:T(8,128)}, u32[]{:S(2)}, u32[]{:S(2)}) collective-permute-start(f32[256,256]{1,0:T(8,128)S(1)} %select_select_fusion), channel_id=1, source_target_pairs={{0,7},{1,0},{2,1},{3,2},{4,3},{5,4},{6,5},{7,6},{8,15},{9,8},{10,9... | collective-permute-start | bytes 786440 | tf_op jit(solution)/shard_map/ppermute | solution.py:29
  42.9 45.7 %all-to-all-start = ((f32[8,128,256]{2,1,0:T(8,128)}), f32[8,128,256]{2,1,0:T(8,128)S(1)}, u32[]{:S(2)}, u32[]{:S(2)}) async-start(f32[8,128,256]{2,1,0:T(8,128)} %bitcast.77), calls=%async_computation | async-start | bytes 2097152 | tf_op jit(solution)/shard_map/all_to_all | solution.py:99
  47.6 39.7 %collective-permute-start.10 = (f32[128,256]{1,0:T(8,128)S(1)}, f32[128,256]{1,0:T(8,128)S(1)}, u32[]{:S(2)}, u32[]{:S(2)}) collective-permute-start(f32[128,256]{1,0:T(8,128)S(1)} %slice.45), channel_id=1, source_target_pairs={{0,2},{1,3},{2,4},{3,5},{4,6},{5,7},{6,0},{7,1},{8,10},{9,11},{10,... | collective-permute-start | bytes 393224 | tf_op jit(solution)/shard_map/ppermute | solution.py:29
  52.8 34.6 %collective-permute-start.9 = (f32[128,256]{1,0:T(8,128)S(1)}, f32[128,256]{1,0:T(8,128)S(1)}, u32[]{:S(2)}, u32[]{:S(2)}) collective-permute-start(f32[128,256]{1,0:T(8,128)S(1)} %slice.44), channel_id=1, source_target_pairs={{0,6},{1,7},{2,0},{3,1},{4,2},{5,3},{6,4},{7,5},{8,14},{9,15},{10,... | collective-permute-start | bytes 393224 | tf_op jit(solution)/shard_map/ppermute | solution.py:29
  56.0 29.4 %collective-permute-start.5 = (f32[256,256]{1,0:T(8,128)}, f32[256,256]{1,0:T(8,128)S(1)}, u32[]{:S(2)}, u32[]{:S(2)}) collective-permute-start(f32[256,256]{1,0:T(8,128)} %collective-permute-done.4), channel_id=1, source_target_pairs={{0,1},{1,2},{2,3},{3,4},{4,5},{5,6},{6,7},{7,0},{8,9},{9,10},{10,1... | collective-permute-start | bytes 786440 | tf_op jit(solution)/shard_map/ppermute | solution.py:29
  59.3 28.1 %collective-permute-start.8 = (f32[256,256]{1,0:T(8,128)}, f32[256,256]{1,0:T(8,128)S(1)}, u32[]{:S(2)}, u32[]{:S(2)}) collective-permute-start(f32[256,256]{1,0:T(8,128)} %collective-permute-done.7), channel_id=1, source_target_pairs={{0,7},{1,0},{2,1},{3,2},{4,3},{5,4},{6,5},{7,6},{8,15},{9,8},{10,9... | collective-permute-start | bytes 786440 | tf_op jit(solution)/shard_map/ppermute | solution.py:29
  91.4 5.6 %collective-permute-start.11 = (f32[768,128]{1,0:T(8,128)}, f32[768,128]{1,0:T(8,128)S(1)}, u32[]{:S(2)}, u32[]{:S(2)}) collective-permute-start(f32[768,128]{1,0:T(8,128)} %pad_maximum_fusion.1), channel_id=1, source_target_pairs={{0,8},{8,0},{1,9},{9,1},{2,10},{10,2},{3,11},{11,3},{4,12},{12,4},... | collective-permute-start | bytes 1179656 | tf_op jit(solution)/shard_map/ppermute | solution.py:77
  151.3 2.0 %copy-start.2 = (f32[256,256]{1,0:T(8,128)S(1)}, f32[256,256]{1,0:T(8,128)}, u32[]{:S(2)}) copy-start(f32[256,256]{1,0:T(8,128)} %copy.11) | copy-start | bytes 786436
  151.3 2.0 %copy-start.3 = (f32[256,2,128]{0,2,1:T(8,128)S(1)}, f32[256,2,128]{0,2,1:T(8,128)}, u32[]{:S(2)}) copy-start(f32[256,2,128]{0,2,1:T(8,128)} %copy.10) | copy-start | bytes 786436
  152.6 1.0 copy-start
